TPU v7x, 512 devices: a whole 4x4x16 slice. The times are simulated.
512 devices in a mesh: tensor: 8 (over x, core), context: 64 (over y, z).
Axes of the slice: x: 4, y: 4, z: 16, core: 2. Of those that a mesh axis runs over, the one named last changes fastest.
Arguments:
- q_proj: bfloat16 [16384, 8192], P('context', 'tensor'), may hold values from -6 to 6
- k_proj: bfloat16 [16384, 8192], P('context', 'tensor'), may hold values from -6 to 6
- v_proj: bfloat16 [16384, 8192], P('context', 'tensor'), may hold values from -6 to 6
- short_filter: bfloat16 [3, 3, 512], P(None, None, 'tensor'), may hold values from -3.5 to 3.5
- residue: float32 [16, 8192], P(None, 'tensor'), may hold values from -1.5 to 1.5
- decay_rate: float32 [16, 8192], P(None, 'tensor'), may hold values from 0.5 to 512
- out_weight: bfloat16 [4096, 8192], P('context', 'tensor'), may hold values from -0.0625 to 0.0625
Outputs:
- projected: bfloat16 [4096, 16384], P('tensor', 'context')
All inputs are finite; a program needn't handle non-finite values.
Results may differ from a plain program's by a relative error of at most 0.02.
Values may be sent and summed in bfloat16 or wider, within the bound.
A program may use at most 128 MiB of HBM per device.

v0:
```python
import jax
import jax.numpy as jnp
import numpy as np
from jax import lax
from jax.sharding import PartitionSpec as P


def passed_along(block, axis, distance):
    devices = range(lax.axis_size(axis))
    route = [(i - distance, i) for i in devices if i - distance in devices]
    return lax.ppermute(block, axis, route)


def prefix(part, axis, combine, identity):
    place = lax.axis_index(axis)
    gathered = jax.tree.map(lambda a: lax.all_gather(a, axis), part)
    state = jax.tree.map(lambda a, e: jnp.zeros_like(a) + jnp.asarray(e, a.dtype), part, identity)

    def one(lap, state):
        return combine(
            state, jax.tree.map(lambda a: lax.dynamic_index_in_dim(a, lap, 0, False), gathered)
        )

    return lax.fori_loop(0, place, one, state)


def short_pass(extended, filters, group_width):
    tap_count = filters.shape[0]
    length_rows, chan_count = extended.shape
    groups = filters.shape[1]
    widened = jnp.broadcast_to(
        filters.astype(jnp.float32)[:, :, None], (tap_count, groups, group_width)
    ).reshape(tap_count, chan_count)
    out_rows = length_rows - tap_count + 1
    running = jnp.zeros((out_rows, chan_count), jnp.float32)
    for offset in range(tap_count):
        begin = tap_count - 1 - offset
        running = running + widened[offset][None, :] * extended[begin : begin + out_rows].astype(
            jnp.float32
        )
    return running


def compose(earlier, later):
    return (earlier[0] * later[0], earlier[1] * later[0] + later[1])


def per_device(q_proj, k_proj, v_proj, short_filter, residue, decay_rate, out_weight):
    row_count, chan_count = q_proj.shape
    short_taps = short_filter.shape[1]
    group_width = chan_count // short_filter.shape[2]
    lead_rows = short_taps - 1
    q_rim, k_rim, v_rim = passed_along(
        (
            q_proj[row_count - lead_rows :],
            k_proj[row_count - lead_rows :],
            v_proj[row_count - lead_rows :],
        ),
        "context",
        1,
    )
    q_feat = short_pass(
        jnp.concatenate([q_rim, q_proj], axis=0), short_filter[0], group_width
    ).astype(jnp.bfloat16)
    k_feat = short_pass(
        jnp.concatenate([k_rim, k_proj], axis=0), short_filter[1], group_width
    ).astype(jnp.bfloat16)
    v_feat = short_pass(
        jnp.concatenate([v_rim, v_proj], axis=0), short_filter[2], group_width
    ).astype(jnp.bfloat16)
    product = (k_feat.astype(jnp.float32) * v_feat.astype(jnp.float32)).astype(jnp.bfloat16)
    sub_len = 16
    sub_count = row_count // sub_len
    decay_step = decay_rate / (row_count * lax.axis_size("context"))
    mode_scale = residue * jnp.sqrt(2.0 * decay_step)
    offsets = jnp.arange(sub_len).astype(jnp.float32)
    intra_kernel = jnp.sum(
        mode_scale[None] * jnp.exp(-decay_step[None] * offsets[:, None, None]), axis=1
    )
    gap_table = np.arange(sub_len)[None, :] - np.arange(sub_len)[:, None]
    one_hot = (gap_table[:, :, None] == np.arange(sub_len)[None, None, :]).astype(np.float32)
    toeplitz = jnp.einsum(
        "sto,oc->stc", jnp.asarray(one_hot), intra_kernel, precision=lax.Precision.HIGHEST
    )
    local_rows = product.astype(jnp.float32).reshape(sub_count, sub_len, chan_count)
    local_part = jnp.einsum("qsc,stc->qtc", local_rows, toeplitz, precision=lax.Precision.HIGHEST)
    tail_powers = jnp.exp(-decay_step[None] * (sub_len - 1 - offsets)[:, None, None])
    sub_ends = jnp.einsum("qsc,smc->qmc", local_rows, tail_powers, precision=lax.Precision.HIGHEST)
    step_decay = jnp.broadcast_to(jnp.exp(-decay_step * sub_len)[None], sub_ends.shape)
    ignored, carried = lax.associative_scan(compose, (step_decay, sub_ends))
    block_state = carried[-1]
    previous = jnp.concatenate([jnp.zeros_like(carried[:1]), carried[:-1]], axis=0)
    block_decay = jnp.exp(-decay_step * row_count)
    unused, incoming = prefix(
        (block_decay, block_state),
        "context",
        compose,
        (jnp.ones_like(block_decay), jnp.zeros_like(block_state)),
    )
    start_decay = jnp.exp(
        -decay_step[None] * (sub_len * jnp.arange(sub_count)).astype(jnp.float32)[:, None, None]
    )
    prior = previous + start_decay * incoming[None]
    lead_powers = jnp.exp(-decay_step[None] * (offsets + 1.0)[:, None, None])
    carried_part = jnp.einsum(
        "qmc,smc->qsc", prior * mode_scale[None], lead_powers, precision=lax.Precision.HIGHEST
    )
    modal_out = (local_part + carried_part).reshape(row_count, chan_count)
    gated = (q_feat.astype(jnp.float32) * modal_out).astype(jnp.bfloat16)
    partial_terms = lax.dot_general(
        lax.all_gather(out_weight, "context", axis=0, tiled=True),
        gated,
        (((1,), (1,)), ((), ())),
        preferred_element_type=jnp.float32,
    )
    return lax.psum_scatter(
        partial_terms.astype(jnp.bfloat16), "tensor", scatter_dimension=0, tiled=True
    )


def solution(mesh):
    return jax.shard_map(
        per_device,
        mesh=mesh,
        in_specs=(
            P("context", "tensor"),
            P("context", "tensor"),
            P("context", "tensor"),
            P(None, None, "tensor"),
            P(None, "tensor"),
            P(None, "tensor"),
            P("context", "tensor"),
        ),
        out_specs=P("tensor", "context"),
        check_vma=False,
    )
```

profile of v0, /device:TPU:8, one launch (start us, length us, event | category | flops | bytes accessed | tf_op | source)
XLA Modules:
  0.0 510.7 jit_solution(3309768442686726028)
XLA Ops:
  6.5 1.6 multiply_exponential_fusion.2
  9.0 3.8 collective-permute-start.1
  13.5 3.8 collective-permute-start.2
  19.2 6.2 %copy.86 = f32[16,16,1024]{1,0,2:T(8,128)} copy(f32[16,16,1024]{2,1,0:T(8,128)S(1)} %multiply_exponential_fusion) | data formatting | bytes 2097152 | tf_op jit(solution)/shard_map/exp | solution.py:87
  26.2 4.7 copy.85
  30.9 12.5 %fusion.15 = f32[1024,16,16]{1,2,0:T(8,128)} fusion(f32[16,16,1024]{1,0,2:T(8,128)} %copy.86, bf16[16,16,1024]{1,0,2:T(8,128)(2,1)} %copy.85), kind=kOutput, calls=%fused_computation.72 | convolution fusion | flops 50331648 | bytes 2621440 | tf_op jit(solution)/shard_map/qsc,smc->qmc/dot_general | solution.py:88
  43.4 5.2 %copy.88 = f32[1024,16,16]{0,1,2:T(8,128)S(1)} copy(f32[1024,16,16]{1,2,0:T(8,128)} %fusion.15) | data formatting | bytes 2097152 | tf_op jit(solution)/shard_map/qsc,smc->qmc/dot_general | solution.py:88
  49.2 3.5 pad.122
  52.8 1.5 slice.359
  55.8 3.8 collective-permute-start
  60.1 3.6 pad.33
  64.0 2.3 slice_add_fusion
  66.3 93.0 %all-gather.9.cloned.1.call-done = f32[1024,1024]{1,0:T(8,128)} async-done(((f32[16,1024]{1,0:T(8,128)}), f32[1024,1024]{1,0:T(8,128)}) %all-gather.9.cloned.1.call-update) | async-done | bytes 4194320 | tf_op jit(solution)/shard_map/all_gather | solution.py:16
  159.3 143.9 %all-gather.5.cloned.1.call-done = f32[64,16,1024]{2,1,0:T(8,128)} async-done(((f32[1,16,1024]{2,1,0:T(8,128)}), f32[64,16,1024]{2,1,0:T(8,128)}) %all-gather.5.cloned.1.call-update) | async-done | bytes 4194320 | tf_op jit(solution)/shard_map/all_gather | solution.py:16
  303.2 15.0 %while.12 = (s32[]{:T(128)}, f32[16,1024]{1,0:T(8,128)S(1)}, s32[]{:T(128)}, f32[64,16,1024]{2,1,0:T(8,128)}, f32[64,16,1024]{2,1,0:T(8,128)}, /*index=5*/s32[]{:T(128)}, s32[]{:T(128)}, s32[]{:T(128)}) while((s32[]{:T(128)}, f32[16,1024]{1,0:T(8,128)S(1)}, s32[]{:T(128)}, f32[64,16,1024]{2,1,0:T(8,128)}, f32[64,16,1024]{2,1,0:T(8,128)}, ...), condition=%wide.region_2.3_spmd, body=%wide.region_1.2_spmd.sunk | while | flops 32773 | bytes 262267 | solution.py:24
  304.1 0.9 bitcast_add_fusion.2
  305.0 0.9 bitcast_add_fusion.2
  306.0 0.9 bitcast_add_fusion.2
  306.9 0.9 bitcast_add_fusion.2
  307.8 0.9 bitcast_add_fusion.2
  318.2 1.9 add_multiply_fusion
  320.1 1.0 fusion.10
  321.1 6.3 %copy.84 = f32[16,16,1024]{0,1,2:T(8,128)} copy(f32[16,16,1024]{2,1,0:T(8,128)S(1)} %fusion.10) | data formatting | bytes 2097152 | tf_op jit(solution)/shard_map/sto,oc->stc/dot_general | solution.py:82
  327.4 6.1 %copy.89 = f32[16,16,1024]{1,0,2:T(8,128)} copy(f32[16,16,1024]{2,1,0:T(8,128)S(1)} %get-tuple-element.76) | data formatting | bytes 2097152 | tf_op jit(solution)/shard_map/exp | solution.py:104
  333.6 6.2 %copy.90 = f32[16,16,1024]{1,0,2:T(8,128)} copy(f32[16,16,1024]{2,1,0:T(8,128)S(1)} %get-tuple-element.72) | data formatting | bytes 2097152 | tf_op jit(solution)/shard_map/mul | solution.py:106
  339.7 14.6 %fusion.14 = f32[1024,16,16]{2,1,0:T(8,128)} fusion(f32[16,16,1024]{0,1,2:T(8,128)} %copy.84, bf16[16,16,1024]{1,0,2:T(8,128)(2,1)} %copy.85), kind=kOutput, calls=%fused_computation.71 | convolution fusion | flops 50331648 | bytes 2621440 | tf_op jit(solution)/shard_map/qsc,stc->qtc/dot_general | solution.py:86
  354.3 18.0 %add_bitcast_fusion = f32[16,16,1024]{0,1,2:T(8,128)} fusion(f32[1024,16,16]{2,1,0:T(8,128)} %fusion.14, f32[16,16,1024]{1,0,2:T(8,128)S(1)} %copy-done, f32[16,16,1024]{1,0,2:T(8,128)} %copy.90), kind=kOutput, calls=%fused_computation.2 | convolution fusion | flops 50593792 | bytes 4194304 | tf_op jit(solution)/shard_map/qmc,smc->qsc/dot_general | solution.py:105
  372.3 5.5 %copy.91 = f32[16,16,1024]{2,1,0:T(8,128)S(1)} copy(f32[16,16,1024]{0,1,2:T(8,128)} %add_bitcast_fusion) | data formatting | bytes 2097152 | tf_op jit(solution)/shard_map/add | solution.py:108
  378.2 79.1 %all-gather.7.cloned.1.call-done = bf16[4096,1024]{1,0:T(8,128)(2,1)} async-done(((bf16[64,1024]{1,0:T(8,128)(2,1)}), bf16[4096,1024]{1,0:T(8,128)(2,1)}) %all-gather.7.cloned.1.call-update) | async-done | bytes 8388624 | tf_op jit(solution)/shard_map/all_gather | solution.py:111
  457.3 7.1 %fusion = bf16[4096,256]{0,1:T(8,128)(2,1)} fusion(bf16[256,1024]{1,0:T(8,128)(2,1)S(1)} %fusion.1, bf16[4096,1024]{1,0:T(8,128)(2,1)} %all-gather.7.cloned.1.call-done), kind=kOutput, calls=%fused_computation.4 | convolution fusion | flops 2148532224 | bytes 11010048 | tf_op jit(solution)/shard_map/dot_general | solution.py:110
  464.5 37.9 %reduce-scatter.2.cloned.1.call-done = bf16[512,256]{0,1:T(8,128)(2,1)} async-done(((bf16[4096,256]{0,1:T(8,128)(2,1)}), bf16[512,256]{0,1:T(8,128)(2,1)}) %reduce-scatter.2.cloned.1.call-update) | async-done | bytes 262160 | tf_op jit(solution)/shard_map/reduce_scatter | solution.py:116
  502.4 1.8 copy.92
  (85 shorter events, 17.3 us)
Async XLA Ops:
  6.5 18.9 %copy-start.2 = (bf16[256,1024]{1,0:T(8,128)(2,1)S(1)}, bf16[256,1024]{1,0:T(8,128)(2,1)}, u32[]{:S(2)}) copy-start(bf16[256,1024]{1,0:T(8,128)(2,1)} %param.11) | copy-start | bytes 1572868
  6.5 18.9 %copy-start.3 = (bf16[256,1024]{1,0:T(8,128)(2,1)S(1)}, bf16[256,1024]{1,0:T(8,128)(2,1)}, u32[]{:S(2)}) copy-start(bf16[256,1024]{1,0:T(8,128)(2,1)} %param.12) | copy-start | bytes 1572868
  6.5 152.7 %all-gather.9.cloned.1.call-start = ((), (), s32[]{:S(2)}) async-start(), calls=%async_computation.4 | async-start | bytes 4259840 | tf_op jit(solution)/shard_map/all_gather | solution.py:16
  8.2 295.0 %all-gather.5.cloned.1.call-start = ((), (), s32[]{:S(2)}) async-start(), calls=%async_computation.1 | async-start | bytes 4259840 | tf_op jit(solution)/shard_map/all_gather | solution.py:16
  9.0 16.4 %collective-permute-start.1 = (bf16[2,1024]{1,0:T(2,128)(2,1)S(1)}, bf16[2,1024]{1,0:T(2,128)(2,1)S(1)}, u32[]{:S(2)}, u32[]{:S(2)}) collective-permute-start(bf16[2,1024]{1,0:T(2,128)(2,1)S(1)} %slice.217), channel_id=1, source_target_pairs={{0,1},{1,2},{2,3},{3,4},{4,5},{5,6},{6,7},{7,8},{8,9},{9,10},{10,1... | collective-permute-start | bytes 12296 | tf_op jit(solution)/shard_map/ppermute | solution.py:11
  13.5 11.9 %collective-permute-start.2 = (bf16[2,1024]{1,0:T(2,128)(2,1)S(1)}, bf16[2,1024]{1,0:T(2,128)(2,1)S(1)}, u32[]{:S(2)}, u32[]{:S(2)}) collective-permute-start(bf16[2,1024]{1,0:T(2,128)(2,1)S(1)} %slice.227), channel_id=1, source_target_pairs={{0,1},{1,2},{2,3},{3,4},{4,5},{5,6},{6,7},{7,8},{8,9},{9,10},{10,1... | collective-permute-start | bytes 12296 | tf_op jit(solution)/shard_map/ppermute | solution.py:11
  43.3 5.3 %copy-start.1 = (f32[16,1024]{1,0:T(8,128)S(1)}, f32[16,1024]{1,0:T(8,128)}, u32[]{:S(2)}) copy-start(f32[16,1024]{1,0:T(8,128)} %param.15) | copy-start | bytes 196612
  49.2 270.9 %copy-start.5 = (f32[16,16,16]{2,1,0:T(8,128)S(1)}, f32[16,16,16]{2,1,0:T(8,128)}, u32[]{:S(2)}) copy-start(f32[16,16,16]{2,1,0:T(8,128)} %constant.42.clone) | copy-start | bytes 49156
  54.3 403.1 %all-gather.7.cloned.1.call-start = ((), (), s32[]{:S(2)}) async-start(), calls=%async_computation.2 | async-start | bytes 8519680 | tf_op jit(solution)/shard_map/all_gather | solution.py:111
  55.0 447.4 %reduce-scatter.2.cloned.1.call-start = ((), (), s32[]{:S(2)}) async-start(), calls=%async_computation.3 | async-start | bytes 2359296 | tf_op jit(solution)/shard_map/reduce_scatter | solution.py:116
  55.8 322.0 %collective-permute-start = (bf16[2,1024]{1,0:T(2,128)(2,1)S(1)}, bf16[2,1024]{1,0:T(2,128)(2,1)S(1)}, u32[]{:S(2)}, u32[]{:S(2)}) collective-permute-start(bf16[2,1024]{1,0:T(2,128)(2,1)S(1)} %slice.207), channel_id=1, source_target_pairs={{0,1},{1,2},{2,3},{3,4},{4,5},{5,6},{6,7},{7,8},{8,9},{9,10},{10,1... | collective-permute-start | bytes 12296 | tf_op jit(solution)/shard_map/ppermute | solution.py:11
  339.7 14.6 %copy-start = (f32[16,16,1024]{1,0,2:T(8,128)S(1)}, f32[16,16,1024]{1,0,2:T(8,128)}, u32[]{:S(2)}) copy-start(f32[16,16,1024]{1,0,2:T(8,128)} %copy.89) | copy-start | bytes 3145732
  372.3 5.5 %copy-start.4 = (bf16[256,1024]{1,0:T(8,128)(2,1)S(1)}, bf16[256,1024]{1,0:T(8,128)(2,1)}, u32[]{:S(2)}) copy-start(bf16[256,1024]{1,0:T(8,128)(2,1)} %param.10) | copy-start | bytes 1572868
Sparse Core Ops, SparseCore 0:
  10.3 148.9 all-gather.8
  162.2 140.8 all-gather.4
  306.1 151.1 all-gather.6
  464.6 37.6 reduce-scatter.1
where the time goes:
time: 514 us; the launch traced here: 511 us
  waiting for transfers between devices  355 us (69%)
  local copies, waits for them, and re-layouts  54.5 us (11%)
  matrix products  53.2 us (10%)
  other arithmetic  22.9 us (4%)
  between operations  13.4 us (3%)
  starting transfers between devices  11.6 us (2%)
    all_gather x2, waiting for transfers between devices, prefix(): gathered = jax.tree.map(lambda a: lax.all_gather(a, axis), part)  237 us
    all_gather x1, waiting for transfers between devices, per_device(): lax.all_gather(out_weight, 'context', axis=0, tiled=True)  79.1 us
    reduce_scatter x1, waiting for transfers between devices, per_device(): lax.psum_scatter(partial_terms.astype(jnp.bfloat16), 'tensor', scatter_di...  37.9 us
    dot_general x1, matrix products, per_device(): jnp.einsum('qmc,smc->qsc', prior * mode_scale[None], lead_powers, precisi...  18 us
    add x22, other arithmetic, compose(): return (earlier[0] * later[0], earlier[1] * later[0] + later[1])  14.8 us
    dot_general x1, matrix products, per_device(): jnp.einsum('qsc,stc->qtc', local_rows, toeplitz, precision=lax.Precision....  14.6 us
    dot_general x1, matrix products, per_device(): jnp.einsum('qsc,smc->qmc', local_rows, tail_powers, precision=lax.Precisi...  12.5 us
    ppermute x3, starting transfers between devices, passed_along(): return lax.ppermute(block, axis, route)  11.4 us
  transfers between devices with their start and end apart: 7, of which 4 were waited for; matrix products, arithmetic and copies ran while one was open for 23% of the time, Pallas kernels for 0%

commit v1 on v0

--- a/solution.py
+++ b/solution.py
@@ -107,8 +107,11 @@
     )
     modal_out = (local_part + carried_part).reshape(row_count, chan_count)
     gated = (q_feat.astype(jnp.float32) * modal_out).astype(jnp.bfloat16)
+    _spread_slabs = lambda m, a_name: jnp.concatenate(
+        lax.all_to_all(jnp.stack(lax.axis_size(a_name) * [m]), a_name, 0, 0), axis=0
+    )
     partial_terms = lax.dot_general(
-        lax.all_gather(out_weight, "context", axis=0, tiled=True),
+        _spread_slabs(out_weight, "context"),
         gated,
         (((1,), (1,)), ((), ())),
         preferred_element_type=jnp.float32,

time: 514 us -> 763 us (1.48)
  waiting for transfers between devices: 355 us -> 582 us
  starting transfers between devices: 11.6 us -> 31 us
    ppermute x3, waiting for transfers between devices: 0.01 us -> 369 us  [passed_along(): return lax.ppermute(block, axis, route)]
    all_gather x2, waiting for transfers between devices: 237 us -> 136 us  [prefix(): gathered = jax.tree.map(lambda a: lax.all_gather(a, axis), part)]
    all_gather x1 -> x0, waiting for transfers between devices: 79.1 us -> none  [per_device(): lax.all_gather(out_weight, 'context', axis=0, tiled=True)]
    reduce_scatter x1, waiting for transfers between devices: 37.9 us -> 77.5 us  [per_device(): lax.psum_scatter(partial_terms.astype(jnp.bfloat16), 'tensor', scatter_di...]
    all_to_all x0 -> x1, starting transfers between devices: none -> 19.1 us  [per_device(): lax.all_to_all(jnp.stack(lax.axis_size(a_name) * [m]), a_name, 0, 0)]
  transfers between devices with their start and end apart: 7 -> 7, of which waited for: 4 -> 4; matrix products, arithmetic and copies ran while one was open for 23% -> 16% of each run, Pallas kernels for 0% -> 0%
where the time goes in v1:
time: 763 us; the launch traced here: 760 us
  waiting for transfers between devices  582 us (76%)
  local copies, waits for them, and re-layouts  58.2 us (8%)
  matrix products  53.1 us (7%)
  starting transfers between devices  31 us (4%)
  other arithmetic  21.2 us (3%)
  between operations  13.5 us (2%)
    ppermute x3, waiting for transfers between devices, passed_along(): return lax.ppermute(block, axis, route)  369 us
    all_gather x2, waiting for transfers between devices, prefix(): gathered = jax.tree.map(lambda a: lax.all_gather(a, axis), part)  136 us
    reduce_scatter x1, waiting for transfers between devices, per_device(): lax.psum_scatter(partial_terms.astype(jnp.bfloat16), 'tensor', scatter_di...  77.5 us
    all_to_all x1, starting transfers between devices, per_device(): lax.all_to_all(jnp.stack(lax.axis_size(a_name) * [m]), a_name, 0, 0)  19.1 us
    dot_general x1, matrix products, per_device(): jnp.einsum('qmc,smc->qsc', prior * mode_scale[None], lead_powers, precisi...  18 us
  transfers between devices with their start and end apart: 7, of which 4 were waited for; matrix products, arithmetic and copies ran while one was open for 16% of the time, Pallas kernels for 0%

profile of v1, /device:TPU:8, one launch (start us, length us, event | category | flops | bytes accessed | tf_op | source)
XLA Modules:
  0.0 759.7 jit_solution(6595331142446124737)
XLA Ops:
  6.5 5.2 stack.2
  11.8 19.1 %all-to-all-start = ((bf16[64,64,1024]{2,1,0:T(8,128)(2,1)}), bf16[64,64,1024]{2,1,0:T(8,128)(2,1)}, u32[]{:S(2)}, u32[]{:S(2)}) async-start(bf16[64,64,1024]{2,1,0:T(8,128)(2,1)} %stack.2), calls=%async_computation | async-start | bytes 16777216 | tf_op jit(solution)/shard_map/all_to_all | solution.py:111
  31.7 3.4 collective-permute-start.1
  35.1 3.4 collective-permute-start.2
  39.7 6.2 copy.86
  45.8 368.7 %collective-permute-done.1 = bf16[2,1024]{1,0:T(2,128)(2,1)S(1)} collective-permute-done((bf16[2,1024]{1,0:T(2,128)(2,1)S(1)}, bf16[2,1024]{1,0:T(2,128)(2,1)S(1)}, u32[]{:S(2)}, u32[]{:S(2)}) %collective-permute-start.1) | collective-permute-done | bytes 4128 | tf_op jit(solution)/shard_map/ppermute | solution.py:11
  415.4 4.7 copy.85
  420.1 12.5 %fusion.15 = f32[1024,16,16]{1,2,0:T(8,128)} fusion(f32[16,16,1024]{1,0,2:T(8,128)} %copy.86, bf16[16,16,1024]{1,0,2:T(8,128)(2,1)} %copy.85), kind=kOutput, calls=%fused_computation.72 | convolution fusion | flops 50331648 | bytes 2621440 | tf_op jit(solution)/shard_map/qsc,smc->qmc/dot_general | solution.py:88
  432.6 5.1 copy.88
  438.4 3.5 pad.122
  441.9 1.5 slice.359
  444.2 5.1 collective-permute-start
  449.8 3.5 pad.33
  453.6 2.3 slice_add_fusion
  455.9 135.7 %all-gather.4.cloned.1.call-done = f32[64,16,1024]{2,1,0:T(8,128)} async-done(((f32[1,16,1024]{2,1,0:T(8,128)}), f32[64,16,1024]{2,1,0:T(8,128)}) %all-gather.4.cloned.1.call-update) | async-done | bytes 4194320 | tf_op jit(solution)/shard_map/all_gather | solution.py:16
  591.5 15.0 %while.12 = (s32[]{:T(128)}, f32[16,1024]{1,0:T(8,128)S(1)}, s32[]{:T(128)}, f32[64,16,1024]{2,1,0:T(8,128)}, f32[64,16,1024]{2,1,0:T(8,128)}, /*index=5*/s32[]{:T(128)}, s32[]{:T(128)}, s32[]{:T(128)}) while((s32[]{:T(128)}, f32[16,1024]{1,0:T(8,128)S(1)}, s32[]{:T(128)}, f32[64,16,1024]{2,1,0:T(8,128)}, f32[64,16,1024]{2,1,0:T(8,128)}, ...), condition=%wide.region_2.3_spmd, body=%wide.region_1.2_spmd.sunk | while | flops 32773 | bytes 262267 | solution.py:24
  592.5 0.9 bitcast_add_fusion.2
  593.4 0.9 bitcast_add_fusion.2
  594.3 0.9 bitcast_add_fusion.2
  595.3 0.9 bitcast_add_fusion.2
  596.2 0.9 bitcast_add_fusion.2
  606.6 1.9 add_multiply_fusion
  608.5 1.0 fusion.10
  609.5 6.3 copy.84
  615.8 6.2 copy.89
  622.0 6.2 copy.90
  628.2 14.6 %fusion.14 = f32[1024,16,16]{2,1,0:T(8,128)} fusion(f32[16,16,1024]{0,1,2:T(8,128)} %copy.84, bf16[16,16,1024]{1,0,2:T(8,128)(2,1)} %copy.85), kind=kOutput, calls=%fused_computation.71 | convolution fusion | flops 50331648 | bytes 2621440 | tf_op jit(solution)/shard_map/qsc,stc->qtc/dot_general | solution.py:86
  642.7 18.0 %add_bitcast_fusion = f32[16,16,1024]{0,1,2:T(8,128)} fusion(f32[1024,16,16]{2,1,0:T(8,128)} %fusion.14, f32[16,16,1024]{1,0,2:T(8,128)S(1)} %copy-done, f32[16,16,1024]{1,0,2:T(8,128)} %copy.90), kind=kOutput, calls=%fused_computation.2 | convolution fusion | flops 50593792 | bytes 4194304 | tf_op jit(solution)/shard_map/qmc,smc->qsc/dot_general | solution.py:105
  660.7 5.5 copy.91
  666.6 7.2 fusion
  673.8 77.5 %reduce-scatter.2.cloned.1.call-done = bf16[512,256]{0,1:T(8,128)(2,1)} async-done(((bf16[4096,256]{0,1:T(8,128)(2,1)}), bf16[512,256]{0,1:T(8,128)(2,1)}) %reduce-scatter.2.cloned.1.call-update) | async-done | bytes 262160 | tf_op jit(solution)/shard_map/reduce_scatter | solution.py:119
  751.3 1.8 copy.92
  (89 shorter events, 15.3 us)
Async XLA Ops:
  11.7 19.1 %copy-start.1 = (f32[16,1024]{1,0:T(8,128)S(1)}, f32[16,1024]{1,0:T(8,128)}, u32[]{:S(2)}) copy-start(f32[16,1024]{1,0:T(8,128)} %param.15) | copy-start | bytes 196612
  11.7 19.2 %copy-start.6 = (f32[16,1024]{1,0:T(8,128)S(1)}, f32[16,1024]{1,0:T(8,128)}, u32[]{:S(2)}) copy-start(f32[16,1024]{1,0:T(8,128)} %param.14) | copy-start | bytes 196612
  11.7 19.9 %copy-start.2 = (bf16[256,1024]{1,0:T(8,128)(2,1)S(1)}, bf16[256,1024]{1,0:T(8,128)(2,1)}, u32[]{:S(2)}) copy-start(bf16[256,1024]{1,0:T(8,128)(2,1)} %param.11) | copy-start | bytes 1572868
  11.7 23.3 %copy-start.3 = (bf16[256,1024]{1,0:T(8,128)(2,1)S(1)}, bf16[256,1024]{1,0:T(8,128)(2,1)}, u32[]{:S(2)}) copy-start(bf16[256,1024]{1,0:T(8,128)(2,1)} %param.12) | copy-start | bytes 1572868
  11.7 26.7 %copy-start.7 = (bf16[3,3,64]{2,1,0:T(4,128)(2,1)S(1)}, bf16[3,3,64]{2,1,0:T(4,128)(2,1)}, u32[]{:S(2)}) copy-start(bf16[3,3,64]{2,1,0:T(4,128)(2,1)} %param.13) | copy-start | bytes 3460
  11.8 654.9 %all-to-all-start = ((bf16[64,64,1024]{2,1,0:T(8,128)(2,1)}), bf16[64,64,1024]{2,1,0:T(8,128)(2,1)}, u32[]{:S(2)}, u32[]{:S(2)}) async-start(bf16[64,64,1024]{2,1,0:T(8,128)(2,1)} %stack.2), calls=%async_computation | async-start | bytes 16777216 | tf_op jit(solution)/shard_map/all_to_all | solution.py:111
  30.8 425.1 %all-gather.6.cloned.1.call-start = ((), (), s32[]{:S(2)}) async-start(), calls=%async_computation.4 | async-start | bytes 4259840 | tf_op jit(solution)/shard_map/all_gather | solution.py:16
  31.6 559.9 %all-gather.4.cloned.1.call-start = ((), (), s32[]{:S(2)}) async-start(), calls=%async_computation.2 | async-start | bytes 4259840 | tf_op jit(solution)/shard_map/all_gather | solution.py:16
  31.7 382.8 %collective-permute-start.1 = (bf16[2,1024]{1,0:T(2,128)(2,1)S(1)}, bf16[2,1024]{1,0:T(2,128)(2,1)S(1)}, u32[]{:S(2)}, u32[]{:S(2)}) collective-permute-start(bf16[2,1024]{1,0:T(2,128)(2,1)S(1)} %slice.217), channel_id=1, source_target_pairs={{0,1},{1,2},{2,3},{3,4},{4,5},{5,6},{6,7},{7,8},{8,9},{9,10},{10,1... | collective-permute-start | bytes 12296 | tf_op jit(solution)/shard_map/ppermute | solution.py:11
  35.1 379.5 %collective-permute-start.2 = (bf16[2,1024]{1,0:T(2,128)(2,1)S(1)}, bf16[2,1024]{1,0:T(2,128)(2,1)S(1)}, u32[]{:S(2)}, u32[]{:S(2)}) collective-permute-start(bf16[2,1024]{1,0:T(2,128)(2,1)S(1)} %slice.227), channel_id=1, source_target_pairs={{0,1},{1,2},{2,3},{3,4},{4,5},{5,6},{6,7},{7,8},{8,9},{9,10},{10,1... | collective-permute-start | bytes 12296 | tf_op jit(solution)/shard_map/ppermute | solution.py:11
  438.4 170.1 %copy-start.5 = (f32[16,16,16]{2,1,0:T(8,128)S(1)}, f32[16,16,16]{2,1,0:T(8,128)}, u32[]{:S(2)}) copy-start(f32[16,16,16]{2,1,0:T(8,128)} %constant.42.clone) | copy-start | bytes 49156
  443.4 308.0 %reduce-scatter.2.cloned.1.call-start = ((), (), s32[]{:S(2)}) async-start(), calls=%async_computation.3 | async-start | bytes 2359296 | tf_op jit(solution)/shard_map/reduce_scatter | solution.py:119
  444.2 222.0 %collective-permute-start = (bf16[2,1024]{1,0:T(2,128)(2,1)S(1)}, bf16[2,1024]{1,0:T(2,128)(2,1)S(1)}, u32[]{:S(2)}, u32[]{:S(2)}) collective-permute-start(bf16[2,1024]{1,0:T(2,128)(2,1)S(1)} %slice.207), channel_id=1, source_target_pairs={{0,1},{1,2},{2,3},{3,4},{4,5},{5,6},{6,7},{7,8},{8,9},{9,10},{10,1... | collective-permute-start | bytes 12296 | tf_op jit(solution)/shard_map/ppermute | solution.py:11
  628.2 14.6 %copy-start = (f32[16,16,1024]{1,0,2:T(8,128)S(1)}, f32[16,16,1024]{1,0,2:T(8,128)}, u32[]{:S(2)}) copy-start(f32[16,16,1024]{1,0,2:T(8,128)} %copy.89) | copy-start | bytes 3145732
  660.7 5.5 copy-start.4
Sparse Core Ops, SparseCore 0:
  34.6 234.4 all-gather.5
  443.5 147.9 all-gather.3
  673.9 77.3 reduce-scatter.1
